TPU v7x, 32 devices: a whole 2x2x4 slice. The times are simulated.
32 devices in a mesh: band: 4 (over y, x), ga: 8 (over z, core).
Axes of the slice: x: 2, y: 2, z: 4, core: 2. Of those that a mesh axis runs over, the one named last changes fastest.
Arguments:
- psi: float32 [4096, 4096], P('band', 'ga'), may hold values from -6 to 6
- lower: float32 [4096, 4096], P('band', 'ga'), as said below
Outputs:
- orthonormal: float32 [4096, 4096], P('band', 'ga')
- block_intersection: float32 [4096, 1024], P('band')
Inputs may be any that keep to these rules, and one draw needn't show every extreme that they name: lower is lower triangular with its diagonal between 1 and 2.
All inputs are finite; a program needn't handle non-finite values.
Results may differ from a plain program's by a relative error of at most 0.00022.
Values sent between devices are 32-bit elements; how exact they have to be, the bound alone decides.
A program may use at most 64 MiB of HBM per device.

v0:
```python
import jax
import jax.numpy as jnp
from jax import lax
from jax.sharding import PartitionSpec as P


def from_root(value, axis, source):
    kept = jnp.where(lax.axis_index(axis) == source, value, 0).astype(value.dtype)
    return lax.psum(kept, axis)


def local(psi, lower):
    myblock = lax.axis_index("band")
    sections = lax.axis_size("band")
    nrows = psi.shape[0]
    width = psi.shape[1]
    full_rows = lax.all_gather(lower, "ga", axis=1, tiled=True)
    own_tile = lax.dynamic_slice_in_dim(full_rows, myblock * nrows, nrows, 1)

    def finish(rhs):
        return jax.scipy.linalg.solve_triangular(own_tile, rhs, lower=True)

    def nothing(rhs):
        return jnp.zeros_like(rhs)

    pieces = 1
    span = width // pieces

    def section(section_idx, carry):
        totals, results = carry
        tile = lax.dynamic_slice_in_dim(full_rows, section_idx * nrows, nrows, 1)
        rhs = psi - totals[0]
        ready = lax.cond(myblock == section_idx, finish, nothing, rhs)
        arrived = from_root(ready, "band", section_idx)
        new_results = [jnp.where(myblock == section_idx, ready, results[0])]
        term = jnp.dot(
            tile, arrived, precision=lax.Precision.HIGHEST, preferred_element_type=jnp.float32
        )
        new_totals = [jnp.where(section_idx < myblock, totals[0] + term, totals[0])]
        return (tuple(new_totals), tuple(new_results))

    blank = tuple((jnp.zeros((nrows, span), jnp.float32) for piece in range(pieces)))
    totals, results = lax.fori_loop(0, sections, section, (blank, blank))
    solved = results[0]
    local_intersection = jnp.dot(
        solved, solved.T, precision=lax.Precision.HIGHEST, preferred_element_type=jnp.float32
    )
    intersection = lax.psum(local_intersection, "ga") / (width * lax.axis_size("ga"))
    return (solved, intersection)


def solution(mesh):
    return jax.shard_map(
        local,
        mesh=mesh,
        in_specs=(P("band", "ga"), P("band", "ga")),
        out_specs=(P("band", "ga"), P("band", None)),
        check_vma=False,
    )
```

profile of v0, /device:TPU:0, one launch (start us, length us, event | category | flops | bytes accessed | tf_op | source)
XLA Modules:
  0.0 1144.7 jit_solution(381688450208989229)
XLA Ops:
  7.9 155.5 %all-gather.2.cloned.1.call-done = f32[1024,4096]{1,0:T(8,128)} async-done(((f32[1024,512]{1,0:T(8,128)}), f32[1024,4096]{1,0:T(8,128)}) %all-gather.2.cloned.1.call-update) | async-done | bytes 16777232 | tf_op jit(solution)/shard_map/all_gather | solution.py:17
  163.4 4.8 constant_dynamic-slice_fusion.1
  168.2 857.6 %while.20 = (s32[]{:T(128)}, f32[1024,512]{1,0:T(8,128)}, f32[1024,512]{1,0:T(8,128)}, s32[]{:T(128)}, f32[1024,4096]{1,0:T(8,128)}, /*index=5*/f32[1024,1024]{1...) while((s32[]{:T(128)}, f32[1024,512]{1,0:T(8,128)}, ...), condition=%wide.region_4.5_spmd.clone, body=%wide.region_0.4_spmd.clone.sunk | while | flops 10074390528 | bytes 73794136 | solution.py:43
  168.4 129.2 %conditional.3 = (f32[1024,512]{1,0:T(8,128)}) conditional(s32[]{:T(128)} %convert_element_type.20, () %tuple.91, (f32[1024,1024]{1,0:T(8,128)}, f32[1024,512]{1,0:T(8,128)}, f32[1024,512]{1,0:T(8,128)S(1)}) %tuple.92), branch_computations={%region_1.0_spmd, %region_2.2_spmd} | conditional | flops 3628269568 | bytes 38142244 | solution.py:33
  168.5 4.7 fusion
  173.2 22.5 %while.19 = (s32[]{:T(128)}, f32[1024,1024]{1,0:T(8,128)}, s32[8,2]{0,1:T(2,128)S(1)}, f32[8,128,128]{2,1,0:T(8,128)S(1)}, s32[]{:T(128)}) while((s32[]{:T(128)}, f32[1024,1024]{1,0:T(8,128)}, s32[8,2]{0,1:T(2,128)S(1)}, f32[8,128,128]{2,1,0:T(8,128)S(1)}, s32[]{:T(128)}) %tuple.95), condition=%wide.while_cond, body=%wide.while_body.sunk | while | flops 2 | bytes 131181 | solution.py:21
  173.8 2.2 bitcast_dynamic-update-slice_fusion.2
  195.7 78.6 %custom-call.3 = f32[8,128,128]{1,2,0:T(8,128)S(1)} custom-call(f32[8,128,128]{2,1,0:T(8,128)S(1)} %get-tuple-element.206), custom_call_target="InvertDiagBlocksLowerTriangular" | custom-call | tf_op jit(solution)/shard_map/while/body/eval_jaxpr/cond/branch_1_fun/jit(_solve_triangular)/triangular_solve | solution.py:21
  294.3 2.2 convolution_subtract_fusion
  297.7 4.3 select_select_fusion.2
  302.0 66.0 %all-reduce.5.cloned.1.call-done = f32[1024,512]{1,0:T(8,128)} async-done(((f32[1024,512]{1,0:T(8,128)}), f32[1024,512]{1,0:T(8,128)}) %all-reduce.5.cloned.1.call-update) | async-done | bytes 2097168 | tf_op jit(solution)/shard_map/while/body/eval_jaxpr/psum | solution.py:9
  368.0 10.3 add_select_fusion.2
  381.7 4.9 select_select_fusion.2
  386.7 197.2 %all-reduce.5.cloned.1.call-done = f32[1024,512]{1,0:T(8,128)} async-done(((f32[1024,512]{1,0:T(8,128)}), f32[1024,512]{1,0:T(8,128)}) %all-reduce.5.cloned.1.call-update) | async-done | bytes 2097168 | tf_op jit(solution)/shard_map/while/body/eval_jaxpr/psum | solution.py:9
  583.9 10.3 add_select_fusion.2
  597.6 4.9 select_select_fusion.2
  602.6 197.1 %all-reduce.5.cloned.1.call-done = f32[1024,512]{1,0:T(8,128)} async-done(((f32[1024,512]{1,0:T(8,128)}), f32[1024,512]{1,0:T(8,128)}) %all-reduce.5.cloned.1.call-update) | async-done | bytes 2097168 | tf_op jit(solution)/shard_map/while/body/eval_jaxpr/psum | solution.py:9
  799.6 10.3 add_select_fusion.2
  813.4 4.9 select_select_fusion.2
  818.3 197.2 %all-reduce.5.cloned.1.call-done = f32[1024,512]{1,0:T(8,128)} async-done(((f32[1024,512]{1,0:T(8,128)}), f32[1024,512]{1,0:T(8,128)}) %all-reduce.5.cloned.1.call-update) | async-done | bytes 2097168 | tf_op jit(solution)/shard_map/while/body/eval_jaxpr/psum | solution.py:9
  1015.5 10.3 add_select_fusion.2
  1025.8 10.3 fusion.40
  1036.1 96.6 %all-reduce.3.cloned.1.call-done = f32[1024,1024]{1,0:T(8,128)} async-done(((f32[1024,1024]{1,0:T(8,128)}), f32[1024,1024]{1,0:T(8,128)}) %all-reduce.3.cloned.1.call-update) | async-done | bytes 4194320 | tf_op jit(solution)/shard_map/psum | solution.py:48
  1132.8 5.0 broadcast_multiply_fusion
  (65 shorter events, 57.5 us)
Async XLA Ops:
  7.2 156.3 %all-gather.2.cloned.1.call-start = ((), (), s32[]{:S(2)}) async-start(), calls=%async_computation | async-start | bytes 18874368 | tf_op jit(solution)/shard_map/all_gather | solution.py:17
  168.2 199.8 %all-reduce.5.cloned.1.call-start = ((), (), s32[]{:S(2)}) async-start(), calls=%async_computation.2 | async-start | bytes 4194304 | tf_op jit(solution)/shard_map/while/body/eval_jaxpr/psum | solution.py:9
  378.3 205.6 %all-reduce.5.cloned.1.call-start = ((), (), s32[]{:S(2)}) async-start(), calls=%async_computation.2 | async-start | bytes 4194304 | tf_op jit(solution)/shard_map/while/body/eval_jaxpr/psum | solution.py:9
  594.1 205.5 %all-reduce.5.cloned.1.call-start = ((), (), s32[]{:S(2)}) async-start(), calls=%async_computation.2 | async-start | bytes 4194304 | tf_op jit(solution)/shard_map/while/body/eval_jaxpr/psum | solution.py:9
  809.9 205.6 %all-reduce.5.cloned.1.call-start = ((), (), s32[]{:S(2)}) async-start(), calls=%async_computation.2 | async-start | bytes 4194304 | tf_op jit(solution)/shard_map/while/body/eval_jaxpr/psum | solution.py:9
  1025.8 107.0 %all-reduce.3.cloned.1.call-start = ((), (), s32[]{:S(2)}) async-start(), calls=%async_computation.1 | async-start | bytes 8388608 | tf_op jit(solution)/shard_map/psum | solution.py:48
Sparse Core Ops, SparseCore 0:
  9.6 153.7 all-gather.1
  302.1 65.8 all-reduce.4
  386.8 197.0 all-reduce.4
  602.7 196.9 all-reduce.4
  818.4 197.0 all-reduce.4
  1036.3 96.4 all-reduce.2
where the time goes:
time: 1150 us; the launch traced here: 1140 us
  waiting for transfers between devices  910 us (79%)
  other arithmetic  115 us (10%)
  matrix products  72.7 us (6%)
  local copies, waits for them, and re-layouts  32 us (3%)
  between operations  14.1 us (1%)
    psum x4, waiting for transfers between devices, from_root(): return lax.psum(kept, axis)  657 us
    all_gather x1, waiting for transfers between devices, local(): full_rows = lax.all_gather(lower, 'ga', axis=1, tiled=True)  155 us
    psum x1, waiting for transfers between devices, local(): lax.psum(local_intersection, 'ga') / (width * lax.axis_size('ga'))  96.6 us
    another operation x3, other arithmetic, finish(): return jax.scipy.linalg.solve_triangular(own_tile, rhs, lower=True)  83.3 us
    dot_general x4, matrix products, section(): jnp.dot(tile, arrived, precision=lax.Precision.HIGHEST, preferred_element...  41.1 us
    another operation x27, local copies, waits for them, and re-layouts  27.2 us
  transfers between devices with their start and end apart: 6, of which 6 were waited for; matrix products, arithmetic and copies ran while one was open for 0% of the time, Pallas kernels for 0%

commit v1 on v0

--- a/solution.py
+++ b/solution.py
@@ -14,7 +14,7 @@
     sections = lax.axis_size("band")
     nrows = psi.shape[0]
     width = psi.shape[1]
-    full_rows = lax.all_gather(lower, "ga", axis=1, tiled=True)
+    full_rows = jnp.concatenate(lax.all_gather(lower, "ga"), axis=1)
     own_tile = lax.dynamic_slice_in_dim(full_rows, myblock * nrows, nrows, 1)
 
     def finish(rhs):

time: 1150 us -> 1160 us (level)
  no operation moved by 1% of the time
where the time goes in v1:
time: 1160 us
  waiting for transfers between devices  912 us (79%)
  other arithmetic  115 us (10%)
  matrix products  72.6 us (6%)
  local copies, waits for them, and re-layouts  42.1 us (4%)
  between operations  14.1 us (1%)
    psum x4, waiting for transfers between devices, from_root(): return lax.psum(kept, axis)  659 us
    all_gather x1, waiting for transfers between devices, local(): full_rows = jnp.concatenate(lax.all_gather(lower, 'ga'), axis=1)  155 us
    psum x1, waiting for transfers between devices, local(): lax.psum(local_intersection, 'ga') / (width * lax.axis_size('ga'))  96.6 us
    another operation x3, other arithmetic, finish(): return jax.scipy.linalg.solve_triangular(own_tile, rhs, lower=True)  83.3 us
    dot_general x4, matrix products, section(): jnp.dot(tile, arrived, precision=lax.Precision.HIGHEST, preferred_element...  41.1 us
    another operation x27, local copies, waits for them, and re-layouts  27.9 us
  transfers between devices with their start and end apart: 6, of which 6 were waited for; matrix products, arithmetic and copies ran while one was open for 0% of the time, Pallas kernels for 0%

profile of v1, /device:TPU:0, one launch (start us, length us, event | category | flops | bytes accessed | tf_op | source)
XLA Modules:
  0.0 1156.7 jit_solution(18079830032886293537)
XLA Ops:
  7.9 155.5 %all-gather.3.cloned.1.call-done = f32[8192,512]{1,0:T(8,128)} async-done(((f32[1024,512]{1,0:T(8,128)}), f32[8192,512]{1,0:T(8,128)}) %all-gather.3.cloned.1.call-update) | async-done | bytes 16777232 | tf_op jit(solution)/shard_map/all_gather | solution.py:17
  163.4 7.2 copy.5
  170.6 2.6 constant_dynamic-slice_fusion.1
  173.3 4.4 copy-done
  177.6 860.2 %while.20 = (s32[]{:T(128)}, f32[1024,512]{1,0:T(8,128)}, f32[1024,512]{1,0:T(8,128)}, s32[]{:T(128)}, f32[1024,4096]{1,0:T(8,128)}, /*index=5*/f32[1024,1024]{1...) while((s32[]{:T(128)}, f32[1024,512]{1,0:T(8,128)}, ...), condition=%wide.region_4.5_spmd.clone, body=%wide.region_0.4_spmd.clone.sunk | while | flops 10074390528 | bytes 73794136 | solution.py:43
  177.9 129.9 %conditional.3 = (f32[1024,512]{1,0:T(8,128)}) conditional(s32[]{:T(128)} %convert_element_type.20, () %tuple.91, (f32[1024,1024]{1,0:T(8,128)}, f32[1024,512]{1,0:T(8,128)}, f32[1024,512]{1,0:T(8,128)S(1)}) %tuple.92), branch_computations={%region_1.0_spmd, %region_2.2_spmd} | conditional | flops 3628269568 | bytes 38142244 | solution.py:33
  177.9 4.7 fusion
  182.6 23.2 %while.19 = (s32[]{:T(128)}, f32[1024,1024]{1,0:T(8,128)}, s32[8,2]{0,1:T(2,128)S(1)}, f32[8,128,128]{2,1,0:T(8,128)S(1)}, s32[]{:T(128)}) while((s32[]{:T(128)}, f32[1024,1024]{1,0:T(8,128)}, s32[8,2]{0,1:T(2,128)S(1)}, f32[8,128,128]{2,1,0:T(8,128)S(1)}, s32[]{:T(128)}) %tuple.95), condition=%wide.while_cond, body=%wide.while_body.sunk | while | flops 2 | bytes 131181 | solution.py:21
  205.8 78.6 %custom-call.3 = f32[8,128,128]{1,2,0:T(8,128)S(1)} custom-call(f32[8,128,128]{2,1,0:T(8,128)S(1)} %get-tuple-element.206), custom_call_target="InvertDiagBlocksLowerTriangular" | custom-call | tf_op jit(solution)/shard_map/while/body/eval_jaxpr/cond/branch_1_fun/jit(_solve_triangular)/triangular_solve | solution.py:21
  307.7 4.3 select_select_fusion.2
  312.1 66.0 %all-reduce.5.cloned.1.call-done = f32[1024,512]{1,0:T(8,128)} async-done(((f32[1024,512]{1,0:T(8,128)}), f32[1024,512]{1,0:T(8,128)}) %all-reduce.5.cloned.1.call-update) | async-done | bytes 2097168 | tf_op jit(solution)/shard_map/while/body/eval_jaxpr/psum | solution.py:9
  378.1 10.3 add_select_fusion.2
  391.8 4.9 select_select_fusion.2
  396.7 197.9 %all-reduce.5.cloned.1.call-done = f32[1024,512]{1,0:T(8,128)} async-done(((f32[1024,512]{1,0:T(8,128)}), f32[1024,512]{1,0:T(8,128)}) %all-reduce.5.cloned.1.call-update) | async-done | bytes 2097168 | tf_op jit(solution)/shard_map/while/body/eval_jaxpr/psum | solution.py:9
  594.6 10.3 add_select_fusion.2
  608.3 4.9 select_select_fusion.2
  613.3 197.7 %all-reduce.5.cloned.1.call-done = f32[1024,512]{1,0:T(8,128)} async-done(((f32[1024,512]{1,0:T(8,128)}), f32[1024,512]{1,0:T(8,128)}) %all-reduce.5.cloned.1.call-update) | async-done | bytes 2097168 | tf_op jit(solution)/shard_map/while/body/eval_jaxpr/psum | solution.py:9
  811.0 10.3 add_select_fusion.2
  824.7 4.9 select_select_fusion.2
  829.7 197.8 %all-reduce.5.cloned.1.call-done = f32[1024,512]{1,0:T(8,128)} async-done(((f32[1024,512]{1,0:T(8,128)}), f32[1024,512]{1,0:T(8,128)}) %all-reduce.5.cloned.1.call-update) | async-done | bytes 2097168 | tf_op jit(solution)/shard_map/while/body/eval_jaxpr/psum | solution.py:9
  1027.5 10.3 add_select_fusion.2
  1037.8 10.3 fusion.40
  1048.2 96.6 %all-reduce.3.cloned.1.call-done = f32[1024,1024]{1,0:T(8,128)} async-done(((f32[1024,1024]{1,0:T(8,128)}), f32[1024,1024]{1,0:T(8,128)}) %all-reduce.3.cloned.1.call-update) | async-done | bytes 4194320 | tf_op jit(solution)/shard_map/psum | solution.py:48
  1144.8 5.0 broadcast_multiply_fusion
  (68 shorter events, 62.5 us)
Async XLA Ops:
  7.2 156.2 %all-gather.3.cloned.1.call-start = ((), (), s32[]{:S(2)}) async-start(), calls=%async_computation.1 | async-start | bytes 18874368 | tf_op jit(solution)/shard_map/all_gather | solution.py:17
  170.6 7.0 copy-start
  177.6 200.4 %all-reduce.5.cloned.1.call-start = ((), (), s32[]{:S(2)}) async-start(), calls=%async_computation.2 | async-start | bytes 4194304 | tf_op jit(solution)/shard_map/while/body/eval_jaxpr/psum | solution.py:9
  388.3 206.3 %all-reduce.5.cloned.1.call-start = ((), (), s32[]{:S(2)}) async-start(), calls=%async_computation.2 | async-start | bytes 4194304 | tf_op jit(solution)/shard_map/while/body/eval_jaxpr/psum | solution.py:9
  604.9 206.1 %all-reduce.5.cloned.1.call-start = ((), (), s32[]{:S(2)}) async-start(), calls=%async_computation.2 | async-start | bytes 4194304 | tf_op jit(solution)/shard_map/while/body/eval_jaxpr/psum | solution.py:9
  821.3 206.2 %all-reduce.5.cloned.1.call-start = ((), (), s32[]{:S(2)}) async-start(), calls=%async_computation.2 | async-start | bytes 4194304 | tf_op jit(solution)/shard_map/while/body/eval_jaxpr/psum | solution.py:9
  1037.8 107.0 %all-reduce.3.cloned.1.call-start = ((), (), s32[]{:S(2)}) async-start(), calls=%async_computation | async-start | bytes 8388608 | tf_op jit(solution)/shard_map/psum | solution.py:48
Sparse Core Ops, SparseCore 0:
  9.6 153.7 all-gather.2
  312.2 65.8 all-reduce.4
  396.8 197.7 all-reduce.4
  613.4 197.5 all-reduce.4
  829.8 197.6 all-reduce.4
  1048.3 96.4 all-reduce.2
